TPU v7x, 512 devices: a whole 4x4x16 slice. The times are simulated.
512 devices in a mesh: row: 32 (over z, x_lo), rep: 16 (over x_hi, y, core).
Axes of the slice: x: 4 (x_hi: 2, x_lo: 2; x = x_hi * 2 + x_lo), y: 4, z: 16, core: 2. Of those that a mesh axis runs over, the one named last changes fastest.
Arguments:
- features: bfloat16 [131072, 256], P(('row', 'rep')), may hold values from -6 to 6
- dense_blocks: bfloat16 [131072, 2, 4096], P('row', None, 'rep'), may hold values from -0.0625 to 0.0625
- thick_neighbour_labels: int32 [32, 2], P('row'), may hold values from 0 to 31, as said below
- tile_source: int32 [32, 16, 64], P('row', 'rep'), may hold values from 0 to 63, as said below
- tile_dest: int32 [32, 16, 64], P('row', 'rep'), may hold values from 0 to 31
- entry_rows: int32 [32, 16, 64, 512], P('row', 'rep'), may hold values from 0 to 127, as said below
- entry_cols: int32 [32, 16, 64, 512], P('row', 'rep'), may hold values from 0 to 127
- edge_strength_list: bfloat16 [32, 16, 64, 512], P('row', 'rep'), may hold values from -0.75 to 0.75
- entry_count: int32 [32, 16, 64], P('row', 'rep'), may hold values from 1 to 512
- weight: bfloat16 [256, 256], replicated, may hold values from -0.375 to 0.375
- out_bias: float32 [256], replicated, may hold values from -3 to 3
Outputs:
- activated: bfloat16 [131072, 256], P(('row', 'rep'))
Inputs may be any that keep to these rules, and one draw needn't show every extreme that they name: `thick_neighbour_labels`: each row block's dense source blocks are distinct and lie within cyclic distance 3 of its own block id. Within one device's list, entries with the same source row block (tile_source // 2) name the same tile. The (entry_rows, entry_cols) pairs of one sparse tile's entries are distinct.
All inputs are finite; a program needn't handle non-finite values.
Results may differ from a plain program's by a relative error of at most 0.0047.
Values may be sent and summed in bfloat16 or wider, within the bound.
A program may use at most 64 MiB of HBM per device.

v0:
```python
import jax
import jax.numpy as jnp
from jax import lax
from jax.sharding import PartitionSpec as P

FEAT = 256
TILE = 128
TILES_DEV = 2


def sparse_terms(
    src_tiles, tile_dest, entry_rows, entry_cols, edge_strength_list, entry_count, dest_tiles
):
    entry_index = lax.broadcasted_iota(jnp.int32, entry_rows.shape, 1)
    active = entry_index < entry_count[:, None]
    weights_live = jnp.where(active, edge_strength_list.astype(jnp.float32), 0.0)
    positions = lax.broadcasted_iota(jnp.int32, (1, 1, TILE), 2)
    row_onehot = (entry_rows[:, :, None] == positions).astype(jnp.bfloat16)
    col_weighted = jnp.where(
        entry_cols[:, :, None] == positions, weights_live[:, :, None], 0.0
    ).astype(jnp.bfloat16)
    tile_mats = jnp.einsum(
        "snr,snc->src", row_onehot, col_weighted, preferred_element_type=jnp.float32
    ).astype(jnp.bfloat16)
    summand_piece = jnp.einsum(
        "src,scf->srf", tile_mats, src_tiles, preferred_element_type=jnp.float32
    )
    target_onehot_mask = (
        tile_dest[None, :] == lax.broadcasted_iota(jnp.int32, (dest_tiles, 1), 0)
    ).astype(jnp.float32)
    placed_entries = jnp.einsum(
        "ou,uwd->owd", target_onehot_mask, summand_piece, precision=lax.Precision.HIGHEST
    )
    return placed_entries.reshape(dest_tiles * TILE, summand_piece.shape[2])


def shards(
    features,
    dense_blocks,
    thick_neighbour_labels,
    tile_source,
    tile_dest,
    entry_rows,
    entry_cols,
    edge_strength_list,
    entry_count,
    weight,
    out_bias,
):
    row_count = lax.axis_size("row")
    own_rows = features.shape[0]
    block_rows = dense_blocks.shape[0]
    block_ids = thick_neighbour_labels[0]
    listed = tile_source[0, 0]
    gathered = lax.all_gather(features, "row", axis=0, tiled=True)
    panel_stack = gathered.reshape(row_count, own_rows, FEAT)
    dense_panels = panel_stack[block_ids]
    src_tiles = gathered.reshape(row_count * TILES_DEV, TILE, FEAT)[listed]
    sparse_part = sparse_terms(
        src_tiles,
        tile_dest[0, 0],
        entry_rows[0, 0],
        entry_cols[0, 0],
        edge_strength_list[0, 0],
        entry_count[0, 0],
        block_rows // TILE,
    )
    dense_part = jnp.einsum(
        "nsc,scf->nf", dense_blocks, dense_panels, preferred_element_type=jnp.float32
    )
    summed = lax.psum_scatter(dense_part + sparse_part, "rep", scatter_dimension=0, tiled=True)
    hidden = summed.astype(jnp.bfloat16)
    projected = jnp.dot(hidden, weight, preferred_element_type=jnp.float32) + out_bias
    return jnp.maximum(projected, 0.0).astype(jnp.bfloat16)


def solution(mesh):
    return jax.shard_map(
        shards,
        mesh=mesh,
        in_specs=(
            P(("row", "rep"), None),
            P("row", None, "rep"),
            P("row", None),
            P("row", "rep", None),
            P("row", "rep", None),
            P("row", "rep", None, None),
            P("row", "rep", None, None),
            P("row", "rep", None, None),
            P("row", "rep", None),
            P(),
            P(),
        ),
        out_specs=P(("row", "rep"), None),
        check_vma=False,
    )
```

profile of v0, /device:TPU:1, one launch (start us, length us, event | category | flops | bytes accessed | tf_op | source)
XLA Modules:
  0.0 315.2 jit_solution(13413633316712423619)
XLA Ops:
  6.5 0.0 copy-start
  6.5 0.0 all-gather.2.cloned.1.call-start
  6.5 0.7 all-gather.2.cloned.1.call-update
  7.3 0.0 reduce-scatter.2.cloned.1.call-start
  7.3 0.7 fusion.18
  8.0 0.7 fusion.17
  8.6 0.9 convert_select_fusion
  9.6 125.1 %all-gather.2.cloned.1.call-done = bf16[8192,256]{1,0:T(8,128)(2,1)} async-done(((bf16[256,256]{1,0:T(8,128)(2,1)}), bf16[8192,256]{1,0:T(8,128)(2,1)}) %all-gather.2.cloned.1.call-update) | async-done | bytes 4194320 | tf_op jit(solution)/shard_map/all_gather | solution.py:55
  134.6 0.0 copy-start.3
  134.6 0.0 copy-start.4
  134.6 5.0 %gather_fusion.1 = bf16[64,128,256]{2,1,0:T(8,128)(2,1)} fusion(bf16[64,128,256]{2,1,0:T(8,128)(2,1)} %bitcast.32, s32[1024]{0:T(1024)S(1)} %pad_clamp_fusion), kind=kCustom, calls=%fused_computation.1 | custom fusion | bytes 8388864 | tf_op jit(solution)/shard_map/gather | solution.py:58
  139.6 0.0 copy-done.3
  139.6 0.0 copy-done.4
  139.6 0.0 copy-start.2
  139.6 22.5 %fusion.9 = f32[64,128,256]{2,1,0:T(8,128)} fusion(bf16[64,128,256]{2,1,0:T(8,128)(2,1)} %gather_fusion.1, bf16[64,512]{1,0:T(8,128)(2,1)S(1)} %convert_select_fusion, s32[64,512]{1,0:T(8,128)S(1)} %bitcast.36, s32[64,512]{1,0:T(8,128)S(1)} %bitcast.37), kind=kOutput, calls=%fused_computation.15 | convolution fusion | flops 1624244224 | bytes 12910592 | tf_op jit(solution)/shard_map/src,scf->srf/dot_general | solution.py:25
  162.2 0.0 copy-done.2
  162.2 11.3 %fusion.1 = f32[32,128,256]{2,0,1:T(8,128)S(1)} fusion(f32[64,128,256]{2,1,0:T(8,128)} %fusion.9, s32[64]{0:T(128)S(1)} %bitcast.35), kind=kOutput, calls=%fused_computation.6 | convolution fusion | flops 805308416 | bytes 12583168 | tf_op jit(solution)/shard_map/ou,uwd->owd/dot_general | solution.py:31
  173.4 4.4 %copy.12 = f32[32,128,256]{2,1,0:T(8,128)} copy(f32[32,128,256]{2,0,1:T(8,128)S(1)} %fusion.1) | data formatting | bytes 8388608 | tf_op jit(solution)/shard_map/ou,uwd->owd/dot_general | solution.py:31
  177.8 2.7 gather_fusion
  180.5 6.7 %fusion.7 = f32[4096,256]{1,0:T(8,128)} fusion(f32[4096,256]{1,0:T(8,128)} %bitcast.31, bf16[2,256,256]{2,1,0:T(8,128)(2,1)S(1)} %gather_fusion, bf16[4096,2,256]{2,1,0:T(2,128)(2,1)} %param.12), kind=kOutput, calls=%fused_computation.13 | convolution fusion | flops 1074790400 | bytes 12845056 | tf_op jit(solution)/shard_map/nsc,scf->nf/dot_general | solution.py:68
  187.3 0.0 copy-start.1
  187.3 0.0 reduce-scatter.2.cloned.1.call-update
  187.3 119.3 %reduce-scatter.2.cloned.1.call-done = f32[256,256]{1,0:T(8,128)} async-done(((f32[4096,256]{1,0:T(8,128)}), f32[256,256]{1,0:T(8,128)}) %reduce-scatter.2.cloned.1.call-update) | async-done | bytes 262160 | tf_op jit(solution)/shard_map/reduce_scatter | solution.py:71
  306.6 0.0 copy-done
  306.6 0.0 copy-done.1
  306.6 1.8 fusion.12
  (2 shorter events, 0.0 us)
Async XLA Ops:
  6.5 300.1 %copy-start = (bf16[256,256]{1,0:T(8,128)(2,1)S(1)}, bf16[256,256]{1,0:T(8,128)(2,1)}, u32[]{:S(2)}) copy-start(bf16[256,256]{1,0:T(8,128)(2,1)} %param.20) | copy-start | bytes 393220
  6.5 128.1 %all-gather.2.cloned.1.call-start = ((), (), s32[]{:S(2)}) async-start(), calls=%async_computation.1 | async-start | bytes 4325376 | tf_op jit(solution)/shard_map/all_gather | solution.py:55
  7.3 299.3 %reduce-scatter.2.cloned.1.call-start = ((), (), s32[]{:S(2)}) async-start(), calls=%async_computation.2 | async-start | bytes 4456448 | tf_op jit(solution)/shard_map/reduce_scatter | solution.py:71
  134.6 5.0 %copy-start.3 = (s32[1,1,64,512]{3,2,1,0:T(8,128)S(1)}, s32[1,1,64,512]{3,2,1,0:T(8,128)}, u32[]{:S(2)}) copy-start(s32[1,1,64,512]{3,2,1,0:T(8,128)} %param.17) | copy-start | bytes 393220
  134.6 5.0 %copy-start.4 = (s32[1,1,64,512]{3,2,1,0:T(8,128)S(1)}, s32[1,1,64,512]{3,2,1,0:T(8,128)}, u32[]{:S(2)}) copy-start(s32[1,1,64,512]{3,2,1,0:T(8,128)} %param.16) | copy-start | bytes 393220
  139.6 22.5 %copy-start.2 = (s32[1,1,64]{2,1,0:T(1,128)S(1)}, s32[1,1,64]{2,1,0:T(1,128)}, u32[]{:S(2)}) copy-start(s32[1,1,64]{2,1,0:T(1,128)} %param.15) | copy-start | bytes 772
  187.3 119.4 %copy-start.1 = (f32[256]{0:T(256)S(1)}, f32[256]{0:T(256)}, u32[]{:S(2)}) copy-start(f32[256]{0:T(256)} %param.21) | copy-start | bytes 3076
Sparse Core Ops, SparseCore 0:
  9.4 125.1 all-gather.1
  187.4 119.1 reduce-scatter.1
where the time goes:
time: 316 us; the launch traced here: 315 us
  waiting for transfers between devices  245 us (78%)
  matrix products  42.3 us (13%)
  between operations  13.4 us (4%)
  local copies, waits for them, and re-layouts  12.1 us (4%)
    all_gather x1, waiting for transfers between devices, shards(): gathered = lax.all_gather(features, 'row', axis=0, tiled=True)  125 us
    reduce_scatter x1, waiting for transfers between devices, shards(): lax.psum_scatter(dense_part + sparse_part, 'rep', scatter_dimension=0, ti...  119 us
    dot_general x1, matrix products, sparse_terms(): jnp.einsum('src,scf->srf', tile_mats, src_tiles, preferred_element_type=j...  22.5 us
    dot_general x1, matrix products, sparse_terms(): jnp.einsum('ou,uwd->owd', target_onehot_mask, summand_piece, precision=la...  11.3 us
    dot_general x1, matrix products, shards(): jnp.einsum('nsc,scf->nf', dense_blocks, dense_panels, preferred_element_t...  6.71 us
  transfers between devices with their start and end apart: 2, of which 2 were waited for; matrix products, arithmetic and copies ran while one was open for 1% of the time, Pallas kernels for 0%

commit v1 on v0

v1 whole, which is shorter than its diff:
```python
import functools

import jax
import jax.numpy as jnp
from jax import lax
from jax.experimental import pallas as pl
from jax.experimental.pallas import tpu as pltpu
from jax.sharding import PartitionSpec as P

FEAT = 256
TILE = 128
NEAR = 2
MESH = pl.DeviceIdType.MESH
HALVES = ((1, 3), (3, 1))


def gather_kernel(
    depth,
    labels,
    counts,
    feat,
    rows_ref,
    cols_ref,
    strength,
    dense_hbm,
    got_out,
    acc_out,
    mats_out,
    near,
    far,
    panels,
    dense_v,
    acc_v,
    mats_v,
    send_sem,
    recv_sem,
    local_sem,
):
    me = lax.axis_index("row")
    z = me // 2
    side = me % 2
    mate = {"row": z * 2 + 1 - side}
    ring = (
        {"row": lax.rem(z + 1, depth) * 2 + side},
        {"row": lax.rem(z + depth - 1, depth) * 2 + side},
    )
    step_sign = (1, -1)
    half = depth // 2

    barrier = pltpu.get_barrier_semaphore()
    for peer in (mate,) + ring:
        pl.semaphore_signal(barrier, inc=1, device_id=peer, device_id_type=MESH)

    dense_in = pltpu.make_async_copy(dense_hbm, dense_v, local_sem.at[0])
    dense_in.start()
    near[NEAR * 2] = feat[...]
    pl.semaphore_wait(barrier, 3)

    def spot(offset, column, tile):
        rows = pl.ds(tile * TILE, TILE)
        offset = depth - half if offset == -half else offset
        if -NEAR <= offset <= NEAR:
            return near.at[(offset + NEAR) * 2 + column, rows]
        place = offset + half - 1 if offset < 0 else offset + half - 2 - 2 * NEAR
        return far.at[place * 2 + column, rows]

    pieces = ((0, 0), (0, 1), (1, 1))
    last = ((half, half - 1), (half - 1, half), (half, half - 1))
    started = []

    def ring_copy(piece, way, step):
        column, tile = pieces[piece]
        sign = step_sign[way]
        here = -sign * (step - 1)
        index = (piece * 2 + way) * half + step - 1
        source = feat.at[pl.ds(tile * TILE, TILE)] if here == 0 and column == 0 else spot(here, column, tile)
        return pltpu.make_async_remote_copy(
            src_ref=source,
            dst_ref=spot(-sign * step, column, tile),
            send_sem=send_sem.at[index],
            recv_sem=recv_sem.at[index],
            device_id=ring[way],
            device_id_type=MESH,
        )

    def mate_copy(offset, tile):
        offset = depth - half if offset == -half else offset
        index = 6 * half + (depth if tile else offset + half - 1)
        source = feat.at[pl.ds(tile * TILE, TILE)] if offset == 0 else spot(offset, 0, tile)
        return pltpu.make_async_remote_copy(
            src_ref=source,
            dst_ref=spot(offset, 1, tile),
            send_sem=send_sem.at[index],
            recv_sem=recv_sem.at[index],
            device_id=mate,
            device_id_type=MESH,
        )

    def begin(copy):
        copy.start()
        started.append(copy)

    positions = lax.broadcasted_iota(jnp.int32, (TILE, rows_ref.shape[1]), 0)
    lanes = lax.broadcasted_iota(jnp.int32, (1, rows_ref.shape[1]), 1)

    def build_mats(first, stop):
        def body(i, carry):
            live = jnp.where(lanes < counts[0, i], strength[pl.ds(i, 1), :], 0.0)
            at_row = jnp.where(positions == rows_ref[pl.ds(i, 1), :], 1.0, 0.0).astype(jnp.bfloat16)
            at_col = jnp.where(positions == cols_ref[pl.ds(i, 1), :], live, 0.0).astype(jnp.bfloat16)
            mats_v[i] = lax.dot_general(
                at_row, at_col, (((1,), (1,)), ((), ())), preferred_element_type=jnp.float32
            ).astype(jnp.bfloat16)
            return carry

        lax.fori_loop(first, stop, body, 0)

    chunk = 256
    chunks = acc_v.shape[0] // chunk

    def dense_part(first, stop):
        def body(i, carry):
            rows = pl.ds(pl.multiple_of(i * chunk, chunk), chunk)
            acc_v[rows, :] = jnp.dot(
                dense_v[rows, :], panels[...], preferred_element_type=jnp.float32
            )
            return carry

        lax.fori_loop(first, stop, body, 0)

    def fetch_panels():
        for slot in range(2):
            label = labels[0, slot]
            offset = jnp.minimum(lax.rem(label // 2 - z + NEAR + depth, depth), 2 * NEAR)
            column = lax.rem(label + side, 2)
            panels[pl.ds(slot * FEAT, FEAT), :] = near[offset * 2 + column]

    begin(mate_copy(0, 1))
    for piece in (0, 1):
        for way in (0, 1):
            begin(ring_copy(piece, way, 1))
    begin(mate_copy(0, 0))
    mate_copy(0, 1).wait_recv()
    for way in (0, 1):
        begin(ring_copy(2, way, 1))

    tiles = mats_v.shape[0]
    early = 3 * (NEAR + 1)
    late = 3 * (half - NEAR - 1)
    slot = 0
    for step in range(1, half + 1):
        for piece in range(3):
            if slot < early:
                build_mats(slot * tiles // early, (slot + 1) * tiles // early)
            else:
                if slot == early:
                    mate_copy(0, 0).wait_recv()
                    for near_step in range(1, NEAR + 1):
                        for sign in step_sign:
                            mate_copy(-sign * near_step, 0).wait_recv()
                    fetch_panels()
                    dense_in.wait()
                dense_part((slot - early) * chunks // late, (slot - early + 1) * chunks // late)
            for way in (0, 1):
                if step <= last[piece][way]:
                    ring_copy(piece, way, step).wait_recv()
                    if step < last[piece][way]:
                        begin(ring_copy(piece, way, step + 1))
                    if piece == 0:
                        begin(mate_copy(-step_sign[way] * step, 0))
            slot += 1
    acc_copy = pltpu.make_async_copy(acc_v, acc_out, local_sem.at[1])
    acc_copy.start()
    mats_copy = pltpu.make_async_copy(mats_v, mats_out, local_sem.at[2])
    mats_copy.start()
    near_copy = pltpu.make_async_copy(near, got_out.at[pl.ds(0, near.shape[0])], local_sem.at[3])
    near_copy.start()
    for offset in range(NEAR + 1, half + 1):
        mate_copy(offset, 0).wait_recv()
        if offset < half:
            mate_copy(-offset, 0).wait_recv()
    far_copy = pltpu.make_async_copy(
        far, got_out.at[pl.ds(near.shape[0], far.shape[0])], local_sem.at[4]
    )
    far_copy.start()
    for copy in started:
        copy.wait_send()
    for copy in (acc_copy, mats_copy, near_copy, far_copy):
        copy.wait()


def gather_and_prepare(features, dense_blocks, labels, counts, rows, cols, strength):
    depth = lax.axis_size("row") // 2
    block_rows = dense_blocks.shape[0]
    tiles = rows.shape[0]
    near = 2 * (2 * NEAR + 1)
    far = 2 * depth - near
    sems = 3 * depth + depth + 1
    vmem = pl.BlockSpec(memory_space=pltpu.VMEM)
    smem = pl.BlockSpec(memory_space=pltpu.SMEM)
    anywhere = pl.BlockSpec(memory_space=pl.ANY)
    return pl.pallas_call(
        functools.partial(gather_kernel, depth),
        out_shape=(
            jax.ShapeDtypeStruct((near + far, FEAT, FEAT), jnp.bfloat16),
            jax.ShapeDtypeStruct((block_rows, FEAT), jnp.float32),
            jax.ShapeDtypeStruct((tiles, TILE, TILE), jnp.bfloat16),
        ),
        in_specs=[smem, smem, vmem, vmem, vmem, vmem, anywhere],
        out_specs=(anywhere, anywhere, anywhere),
        scratch_shapes=[
            pltpu.VMEM((near, FEAT, FEAT), jnp.bfloat16),
            pltpu.VMEM((far, FEAT, FEAT), jnp.bfloat16),
            pltpu.VMEM((2 * FEAT, FEAT), jnp.bfloat16),
            pltpu.VMEM(dense_blocks.shape, jnp.bfloat16),
            pltpu.VMEM((block_rows, FEAT), jnp.float32),
            pltpu.VMEM((tiles, TILE, TILE), jnp.bfloat16),
            pltpu.SemaphoreType.DMA((sems,)),
            pltpu.SemaphoreType.DMA((sems,)),
            pltpu.SemaphoreType.DMA((5,)),
        ],
        compiler_params=pltpu.CompilerParams(collective_id=0, has_side_effects=True),
        name="gather_and_prepare",
    )(labels, counts, features, rows, cols, strength, dense_blocks)


def place_kernel(source, dest, got, mats, acc_hbm, out, acc, sem):
    copy = pltpu.make_async_copy(acc_hbm, acc, sem)
    copy.start()
    copy.wait()

    def body(i, carry):
        rows = pl.ds(pl.multiple_of(dest[0, i] * TILE, TILE), TILE)
        acc[rows, :] += jnp.dot(
            mats[i], got[source[0, i]], preferred_element_type=jnp.float32
        )
        return carry

    lax.fori_loop(0, mats.shape[0], body, 0)
    out[...] = acc[...].astype(jnp.bfloat16)


def place_tiles(source, dest, got, mats, acc):
    vmem = pl.BlockSpec(memory_space=pltpu.VMEM)
    smem = pl.BlockSpec(memory_space=pltpu.SMEM)
    return pl.pallas_call(
        place_kernel,
        out_shape=jax.ShapeDtypeStruct(acc.shape, jnp.bfloat16),
        in_specs=[smem, smem, vmem, vmem, pl.BlockSpec(memory_space=pl.ANY)],
        out_specs=vmem,
        scratch_shapes=[pltpu.VMEM(acc.shape, jnp.float32), pltpu.SemaphoreType.DMA],
        name="place_tiles",
    )(source, dest, got, mats, acc)


def scatter_kernel(
    part, weight, bias, out, from_core, sum_core, from_one, sum_one, from_two, sum_two, from_x, send_sem, recv_sem
):
    me = lax.axis_index("rep")
    core = me % 2
    y = (me // 2) % 4
    x = me // 8

    def rep_of(xx, yy, cc):
        return (xx * 4 + yy) * 2 + cc

    flips = (y, y + 1 - 2 * (y % 2), (y + 2) % 4, 3 - y)
    mate = {"rep": rep_of(x, y, 1 - core)}
    y_peer = {1: {"rep": rep_of(x, flips[1], core)}, 3: {"rep": rep_of(x, flips[3], core)}}
    x_peer = {"rep": rep_of(1 - x, y, core)}
    barrier = pltpu.get_barrier_semaphore()
    for peer in (mate, y_peer[1], y_peer[3], x_peer):
        pl.semaphore_signal(barrier, inc=1, device_id=peer, device_id_type=MESH)
    pl.semaphore_wait(barrier, 4)

    def piece(h, q, t, cc):
        xx = x if q == 0 else 1 - x
        first = rep_of(xx, flips[t], cc) * (2 * TILE) + h * TILE
        return part.at[pl.ds(pl.multiple_of(first, TILE), TILE)]

    def number(h, q, t):
        return (h * 2 + q) * 4 + t

    def remote(source, target, index, peer):
        return pltpu.make_async_remote_copy(
            src_ref=source,
            dst_ref=target,
            send_sem=send_sem.at[index],
            recv_sem=recv_sem.at[index],
            device_id=peer,
            device_id_type=MESH,
        )

    def core_copy(h, q, t):
        n = number(h, q, t)
        return remote(piece(h, q, t, 1 - core), from_core.at[n], n, mate)

    def one_copy(h, q, t):
        way = HALVES[h][0]
        arrives = {1: {1: 0, 2: 3}, 3: {3: 0, 2: 1}}[way][t]
        slot = (h * 2 + q) * 2 + (0 if arrives == 0 else 1)
        return remote(sum_core.at[slot], from_one.at[slot], 16 + slot, y_peer[way])

    def two_copy(h, q):
        slot = h * 2 + q
        return remote(sum_two.at[slot], from_two.at[slot], 24 + slot, y_peer[HALVES[h][1]])

    def x_copy(h):
        return remote(sum_one.at[h], from_x.at[h], 28 + h, x_peer)

    def wide(ref):
        return ref[...].astype(jnp.float32)

    started = []

    def begin(copy):
        copy.start()
        started.append(copy)

    first_order = [(h, q, t) for t in (0, 1) for q in (1, 0) for h in (0, 1)]
    sends_one = [(h, q, 2 if k == 0 else HALVES[h][0]) for (h, q, k) in first_order]
    stays = [(h, q, HALVES[h][1]) for q in (1, 0) for h in (0, 1)]
    ends = [(h, q, 0) for q in (1, 0) for h in (0, 1)]
    for key in sends_one + stays + ends:
        begin(core_copy(*key))
    for h, q, t in sends_one:
        copy = one_copy(h, q, t)
        core_copy(h, q, t).wait_recv()
        way = HALVES[h][0]
        slot = (h * 2 + q) * 2 + (0 if t == way else 1)
        sum_core[slot] = (
            wide(piece(h, q, t, core)) + wide(from_core.at[number(h, q, t)])
        ).astype(jnp.bfloat16)
        begin(copy)
    for h, q, t in stays:
        core_copy(h, q, t).wait_recv()
        one_copy(h, q, 2).wait_recv()
        sum_two[h * 2 + q] = (
            wide(piece(h, q, t, core))
            + wide(from_core.at[number(h, q, t)])
            + wide(from_one.at[(h * 2 + q) * 2 + 1])
        ).astype(jnp.bfloat16)
        begin(two_copy(h, q))

    def total(h, q):
        core_copy(h, q, 0).wait_recv()
        one_copy(h, q, HALVES[h][0]).wait_recv()
        two_copy(h, q).wait_recv()
        return (
            wide(piece(h, q, 0, core))
            + wide(from_core.at[number(h, q, 0)])
            + wide(from_one.at[(h * 2 + q) * 2])
            + wide(from_two.at[h * 2 + q])
        )

    for h in (0, 1):
        sum_one[h] = total(h, 1).astype(jnp.bfloat16)
        begin(x_copy(h))
    for h in (0, 1):
        own = total(h, 0)
        x_copy(h).wait_recv()
        hidden = (own + wide(from_x.at[h])).astype(jnp.bfloat16)
        projected = jnp.dot(hidden, weight[...], preferred_element_type=jnp.float32) + bias[...]
        out[pl.ds(h * TILE, TILE), :] = jnp.maximum(projected, 0.0).astype(jnp.bfloat16)
    for copy in started:
        copy.wait_send()


def scatter_and_project(part, weight, bias):
    vmem = pl.BlockSpec(memory_space=pltpu.VMEM)

    def tiles(n):
        return pltpu.VMEM((n, TILE, FEAT), jnp.bfloat16)

    return pl.pallas_call(
        scatter_kernel,
        out_shape=jax.ShapeDtypeStruct((2 * TILE, FEAT), jnp.bfloat16),
        in_specs=[vmem, vmem, vmem],
        out_specs=vmem,
        scratch_shapes=[
            tiles(16),
            tiles(8),
            tiles(8),
            tiles(2),
            tiles(4),
            tiles(4),
            tiles(2),
            pltpu.SemaphoreType.DMA((30,)),
            pltpu.SemaphoreType.DMA((30,)),
        ],
        compiler_params=pltpu.CompilerParams(collective_id=1, has_side_effects=True),
        name="scatter_and_project",
    )(part, weight, bias)


def shards(
    features,
    dense_blocks,
    thick_neighbour_labels,
    tile_source,
    tile_dest,
    entry_rows,
    entry_cols,
    edge_strength_list,
    entry_count,
    weight,
    out_bias,
):
    depth = lax.axis_size("row") // 2
    block_rows = dense_blocks.shape[0]
    me = lax.axis_index("row")
    got, acc, mats = gather_and_prepare(
        features,
        dense_blocks.reshape(block_rows, 2 * FEAT),
        thick_neighbour_labels,
        entry_count[0],
        entry_rows[0, 0],
        entry_cols[0, 0],
        edge_strength_list[0, 0].astype(jnp.float32),
    )
    half = depth // 2
    block = tile_source[0] // 2
    offset = (block // 2 - me // 2 + half - 1 + depth) % depth - (half - 1)
    near_place = offset + NEAR
    far_place = 2 * NEAR + 1 + jnp.where(offset < 0, offset + half - 1, offset + half - 2 - 2 * NEAR)
    place = jnp.where(jnp.abs(offset) <= NEAR, near_place, far_place)
    source = (place * 2 + (block + me) % 2) * 2 + tile_source[0] % 2
    part = place_tiles(
        source.astype(jnp.int32),
        tile_dest[0],
        got.reshape(4 * depth, TILE, FEAT),
        mats,
        acc,
    )
    return scatter_and_project(part, weight, out_bias.reshape(1, FEAT))


def solution(mesh):
    return jax.shard_map(
        shards,
        mesh=mesh,
        in_specs=(
            P(("row", "rep"), None),
            P("row", None, "rep"),
            P("row", None),
            P("row", "rep", None),
            P("row", "rep", None),
            P("row", "rep", None, None),
            P("row", "rep", None, None),
            P("row", "rep", None, None),
            P("row", "rep", None),
            P(),
            P(),
        ),
        out_specs=P(("row", "rep"), None),
        check_vma=False,
    )
```

time: 316 us -> 104 us (0.33)
  waiting for transfers between devices: 245 us -> 0 us
  Pallas kernels: 0 us -> 94.3 us
  matrix products: 42.3 us -> 0 us
  between operations: 13.4 us -> 0.03 us
  local copies, waits for them, and re-layouts: 12.1 us -> 6.46 us
    all_gather x1 -> x0, waiting for transfers between devices: 125 us -> none  [shards(): gathered = lax.all_gather(features, 'row', axis=0, tiled=True)]
    reduce_scatter x1 -> x0, waiting for transfers between devices: 119 us -> none  [shards(): lax.psum_scatter(dense_part + sparse_part, 'rep', scatter_dimension=0, ti...]
    pallas_call x0 -> x3, Pallas kernels: none -> 94.3 us  [the longest x1 51.3 us: gather_and_prepare(): pl.pallas_call(functools.partial(gather_kernel, depth), out_shape=(jax.Sh...]
    dot_general x4 -> x0, matrix products: 42.3 us -> none  [the longest x1 22.5 us: sparse_terms(): jnp.einsum('src,scf->srf', tile_mats, src_tiles, preferred_element_type=j...]
    gather x2 -> x0, local copies, waits for them, and re-layouts: 7.73 us -> none  [the longest x1 4.98 us: shards(): src_tiles = gathered.reshape(row_count * TILES_DEV, TILE, FEAT)[listed]]
    unnamed x10 -> x2, local copies, waits for them, and re-layouts: 0.02 us -> 6.46 us
    dot_general x1 -> x0, local copies, waits for them, and re-layouts: 4.37 us -> none  [sparse_terms(): jnp.einsum('ou,uwd->owd', target_onehot_mask, summand_piece, precision=la...]
  transfers between devices with their start and end apart: 2 -> 0, of which waited for: 2 -> 0; matrix products, arithmetic and copies ran while one was open for 1% -> 0% of each run, Pallas kernels for 0% -> 0%
where the time goes in v1:
time: 104 us
  Pallas kernels  94.3 us (91%)
  local copies, waits for them, and re-layouts  6.46 us (6%)
  other arithmetic  2.78 us (3%)
    pallas_call x1, Pallas kernels, gather_and_prepare(): pl.pallas_call(functools.partial(gather_kernel, depth), out_shape=(jax.Sh...  51.3 us
    pallas_call x1, Pallas kernels, scatter_and_project(): pl.pallas_call(scatter_kernel, out_shape=jax.ShapeDtypeStruct((2 * TILE,...  26.6 us
    pallas_call x1, Pallas kernels, place_tiles(): pl.pallas_call(place_kernel, out_shape=jax.ShapeDtypeStruct(acc.shape, jn...  16.4 us
    unnamed x2, local copies, waits for them, and re-layouts  6.46 us

profile of v1, /device:TPU:1, one launch (start us, length us, event | category | flops | bytes accessed | tf_op | source)
XLA Modules:
  0.0 103.5 jit_solution(405185379337242326)
XLA Ops:
  0.0 1.3 %fusion.1.source = s32[1,64]{1,0:T(1,128)} fusion(s32[1,1,64]{2,1,0:T(1,128)} %param.14, s32[]{:T(128)S(6)} %axis_index.15, s32[]{:T(128)S(6)} %select_n.91), kind=kLoop, calls=%fused_computation.19 | loop fusion | flops 4544 | bytes 520 | tf_op jit(solution)/shard_map/add | solution.py:427
  1.3 1.5 %bitcast_convert_fusion.strength = f32[64,512]{1,0:T(8,128)} fusion(bf16[1,1,64,512]{3,2,1,0:T(8,128)(2,1)} %param.18), kind=kLoop, calls=%fused_computation | loop fusion | flops 32768 | bytes 196608 | tf_op jit(solution)/shard_map/convert_element_type | solution.py:419
  2.8 4.9 %copy.12 = bf16[512,8,2,256]{3,1,2,0:T(8,128)(2,1)} copy(bf16[512,8,2,256]{3,2,1,0:T(2,128)(2,1)} %bitcast.26) | data formatting | bytes 8388608
  7.7 51.3 %gather_and_prepare.1 = (bf16[32,256,256]{2,1,0:T(8,128)(2,1)}, f32[4096,256]{1,0:T(8,128)}, bf16[64,128,128]{2,1,0:T(8,128)(2,1)}) custom-call(s32[1,2]{1,0:T(1,128)} %labels.1, s32[1,64]{1,0:T(1,128)} %bitcast.30, bf16[256,256]{1,0:T(8,128)(2,1)} %feat.1, s32[64,512]{1,0:T(8,128)} %bitcast.27, s32[64,512]{1,0:T(8,128)} %bitcast.28, ...), custom_call_target="tpu_custom_call" | custom-call | tf_op jit(solution)/shard_map/gather_and_prepare/pallas_call | solution.py:202
  59.0 16.4 %place_tiles.1.part = bf16[4096,256]{1,0:T(8,128)(2,1)} custom-call(s32[1,64]{1,0:T(1,128)} %fusion.1.source, s32[1,64]{1,0:T(1,128)} %bitcast.31, bf16[64,128,256]{2,1,0:T(8,128)(2,1)} %bitcast.25, bf16[64,128,128]{2,1,0:T(8,128)(2,1)} %get-tuple-element.9.mats, f32[4096,256]{1,0:T(8,128)} %get-tuple-element.10.acc_hbm), custom_call_target="tpu_custom_call" | custom-call | tf_op jit(solution)/shard_map/place_tiles/pallas_call | solution.py:246
  75.4 26.6 %scatter_and_project.1 = bf16[256,256]{1,0:T(8,128)(2,1)} custom-call(bf16[4096,256]{1,0:T(8,128)(2,1)} %place_tiles.1.part, bf16[256,256]{1,0:T(8,128)(2,1)} %weight.1, f32[1,256]{1,0:T(1,128)} %bitcast.29), custom_call_target="tpu_custom_call" | custom-call | tf_op jit(solution)/shard_map/scatter_and_project/pallas_call | solution.py:375
  102.0 1.6 %copy.14 = bf16[256,256]{1,0:T(8,128)(2,1)} copy(bf16[256,256]{1,0:T(8,128)(2,1)} %scatter_and_project.1) | data formatting | bytes 262144

commit v2 on v1

--- a/solution.py
+++ b/solution.py
@@ -10,6 +10,7 @@
 FEAT = 256
 TILE = 128
 NEAR = 2
+BY_MATE = (4, 6)
 MESH = pl.DeviceIdType.MESH
 HALVES = ((1, 3), (3, 1))
 
@@ -21,20 +22,16 @@
     feat,
     rows_ref,
     cols_ref,
-    strength,
-    dense_hbm,
-    got_out,
-    acc_out,
-    mats_out,
-    near,
-    far,
-    panels,
+    strength_in,
     dense_v,
+    got,
     acc_v,
     mats_v,
+    panels,
+    mixed,
+    strength,
     send_sem,
     recv_sem,
-    local_sem,
 ):
     me = lax.axis_index("row")
     z = me // 2
@@ -51,18 +48,14 @@
     for peer in (mate,) + ring:
         pl.semaphore_signal(barrier, inc=1, device_id=peer, device_id_type=MESH)
 
-    dense_in = pltpu.make_async_copy(dense_hbm, dense_v, local_sem.at[0])
-    dense_in.start()
-    near[NEAR * 2] = feat[...]
+    got[2 * (half - 1)] = feat[...]
+    strength[...] = strength_in[...].astype(jnp.float32)
     pl.semaphore_wait(barrier, 3)
 
     def spot(offset, column, tile):
         rows = pl.ds(tile * TILE, TILE)
         offset = depth - half if offset == -half else offset
-        if -NEAR <= offset <= NEAR:
-            return near.at[(offset + NEAR) * 2 + column, rows]
-        place = offset + half - 1 if offset < 0 else offset + half - 2 - 2 * NEAR
-        return far.at[place * 2 + column, rows]
+        return got.at[(offset + half - 1) * 2 + column, rows]
 
     pieces = ((0, 0), (0, 1), (1, 1))
     last = ((half, half - 1), (half - 1, half), (half, half - 1))
@@ -85,7 +78,11 @@
 
     def mate_copy(offset, tile):
         offset = depth - half if offset == -half else offset
-        index = 6 * half + (depth if tile else offset + half - 1)
+        index = 6 * half + offset + half - 1
+        if tile:
+            index = 7 * half + depth // 2
+            if offset:
+                index += 1 + 2 * BY_MATE.index(abs(offset)) + (offset > 0)
         source = feat.at[pl.ds(tile * TILE, TILE)] if offset == 0 else spot(offset, 0, tile)
         return pltpu.make_async_remote_copy(
             src_ref=source,
@@ -121,9 +118,15 @@
     def dense_part(first, stop):
         def body(i, carry):
             rows = pl.ds(pl.multiple_of(i * chunk, chunk), chunk)
-            acc_v[rows, :] = jnp.dot(
-                dense_v[rows, :], panels[...], preferred_element_type=jnp.float32
+            both = jnp.dot(
+                dense_v[rows].reshape(2 * chunk, FEAT), panels[...], preferred_element_type=jnp.float32
             )
+            for lane in range(4):
+                mixed[lane] = both[:, lane * TILE : (lane + 1) * TILE]
+            for lane in range(2):
+                acc_v[rows, pl.ds(lane * TILE, TILE)] = (
+                    mixed[lane, pl.ds(0, chunk, stride=2), :] + mixed[lane + 2, pl.ds(1, chunk, stride=2), :]
+                )
             return carry
 
         lax.fori_loop(first, stop, body, 0)
@@ -131,9 +134,12 @@
     def fetch_panels():
         for slot in range(2):
             label = labels[0, slot]
-            offset = jnp.minimum(lax.rem(label // 2 - z + NEAR + depth, depth), 2 * NEAR)
-            column = lax.rem(label + side, 2)
-            panels[pl.ds(slot * FEAT, FEAT), :] = near[offset * 2 + column]
+            wanted = lax.rem(label // 2 - z + NEAR + depth, depth) * 2 + lax.rem(label + side, 2)
+            first = 2 * (half - 1 - NEAR)
+            panel = got[first]
+            for k in range(1, 2 * (2 * NEAR + 1)):
+                panel = jnp.where(wanted == k, got[first + k], panel)
+            panels[:, pl.ds(slot * FEAT, FEAT)] = panel
 
     begin(mate_copy(0, 1))
     for piece in (0, 1):
@@ -159,96 +165,93 @@
                         for sign in step_sign:
                             mate_copy(-sign * near_step, 0).wait_recv()
                     fetch_panels()
-                    dense_in.wait()
                 dense_part((slot - early) * chunks // late, (slot - early + 1) * chunks // late)
             for way in (0, 1):
                 if step <= last[piece][way]:
-                    ring_copy(piece, way, step).wait_recv()
-                    if step < last[piece][way]:
+                    away = -step_sign[way] * step
+                    if piece == 2 and step in BY_MATE:
+                        mate_copy(away, 1).wait_recv()
+                    else:
+                        ring_copy(piece, way, step).wait_recv()
+                    if step < last[piece][way] and not (piece == 2 and step + 1 in BY_MATE):
                         begin(ring_copy(piece, way, step + 1))
-                    if piece == 0:
-                        begin(mate_copy(-step_sign[way] * step, 0))
+                    if piece == 0 or piece == 1 and step in BY_MATE:
+                        begin(mate_copy(away, piece))
             slot += 1
-    acc_copy = pltpu.make_async_copy(acc_v, acc_out, local_sem.at[1])
-    acc_copy.start()
-    mats_copy = pltpu.make_async_copy(mats_v, mats_out, local_sem.at[2])
-    mats_copy.start()
-    near_copy = pltpu.make_async_copy(near, got_out.at[pl.ds(0, near.shape[0])], local_sem.at[3])
-    near_copy.start()
     for offset in range(NEAR + 1, half + 1):
         mate_copy(offset, 0).wait_recv()
         if offset < half:
             mate_copy(-offset, 0).wait_recv()
-    far_copy = pltpu.make_async_copy(
-        far, got_out.at[pl.ds(near.shape[0], far.shape[0])], local_sem.at[4]
-    )
-    far_copy.start()
     for copy in started:
         copy.wait_send()
-    for copy in (acc_copy, mats_copy, near_copy, far_copy):
-        copy.wait()
 
 
 def gather_and_prepare(features, dense_blocks, labels, counts, rows, cols, strength):
     depth = lax.axis_size("row") // 2
     block_rows = dense_blocks.shape[0]
     tiles = rows.shape[0]
-    near = 2 * (2 * NEAR + 1)
-    far = 2 * depth - near
-    sems = 3 * depth + depth + 1
+    sems = 3 * depth + depth + 1 + 2 * len(BY_MATE)
     vmem = pl.BlockSpec(memory_space=pltpu.VMEM)
     smem = pl.BlockSpec(memory_space=pltpu.SMEM)
-    anywhere = pl.BlockSpec(memory_space=pl.ANY)
     return pl.pallas_call(
         functools.partial(gather_kernel, depth),
         out_shape=(
-            jax.ShapeDtypeStruct((near + far, FEAT, FEAT), jnp.bfloat16),
+            jax.ShapeDtypeStruct((2 * depth, FEAT, FEAT), jnp.bfloat16),
             jax.ShapeDtypeStruct((block_rows, FEAT), jnp.float32),
             jax.ShapeDtypeStruct((tiles, TILE, TILE), jnp.bfloat16),
         ),
-        in_specs=[smem, smem, vmem, vmem, vmem, vmem, anywhere],
-        out_specs=(anywhere, anywhere, anywhere),
+        in_specs=[smem, smem, vmem, vmem, vmem, vmem, vmem],
+        out_specs=(vmem, vmem, vmem),
         scratch_shapes=[
-            pltpu.VMEM((near, FEAT, FEAT), jnp.bfloat16),
-            pltpu.VMEM((far, FEAT, FEAT), jnp.bfloat16),
-            pltpu.VMEM((2 * FEAT, FEAT), jnp.bfloat16),
-            pltpu.VMEM(dense_blocks.shape, jnp.bfloat16),
-            pltpu.VMEM((block_rows, FEAT), jnp.float32),
-            pltpu.VMEM((tiles, TILE, TILE), jnp.bfloat16),
+            pltpu.VMEM((FEAT, 2 * FEAT), jnp.bfloat16),
+            pltpu.VMEM((4, 2 * FEAT, TILE), jnp.float32),
+            pltpu.VMEM(rows.shape, jnp.float32),
             pltpu.SemaphoreType.DMA((sems,)),
             pltpu.SemaphoreType.DMA((sems,)),
-            pltpu.SemaphoreType.DMA((5,)),
         ],
-        compiler_params=pltpu.CompilerParams(collective_id=0, has_side_effects=True),
+        compiler_params=pltpu.CompilerParams(collective_id=0, has_side_effects=True, vmem_limit_bytes=20 * 2**20),
         name="gather_and_prepare",
     )(labels, counts, features, rows, cols, strength, dense_blocks)
 
 
-def place_kernel(source, dest, got, mats, acc_hbm, out, acc, sem):
-    copy = pltpu.make_async_copy(acc_hbm, acc, sem)
-    copy.start()
-    copy.wait()
-
-    def body(i, carry):
-        rows = pl.ds(pl.multiple_of(dest[0, i] * TILE, TILE), TILE)
-        acc[rows, :] += jnp.dot(
-            mats[i], got[source[0, i]], preferred_element_type=jnp.float32
-        )
+def place_kernel(depth, source, dest, got, mats, dense, out, acc):
+    acc[...] = jnp.zeros_like(acc)
+    me = lax.axis_index("row")
+    half = depth // 2
+    group = 4
+
+    def spot(i):
+        listed = source[0, i]
+        block = lax.div(listed, 2)
+        offset = lax.rem(lax.div(block, 2) - lax.div(me, 2) + half - 1 + depth, depth)
+        return (offset * 2 + lax.rem(block + me, 2)) * 2 + lax.rem(listed, 2)
+
+    def body(g, carry):
+        terms = [
+            jnp.dot(
+                mats[g * group + k], got[spot(g * group + k)], preferred_element_type=jnp.float32
+            )
+            for k in range(group)
+        ]
+        for k in range(group):
+            rows = pl.ds(pl.multiple_of(dest[0, g * group + k] * TILE, TILE), TILE)
+            acc[rows, :] += terms[k]
         return carry
 
-    lax.fori_loop(0, mats.shape[0], body, 0)
-    out[...] = acc[...].astype(jnp.bfloat16)
+    lax.fori_loop(0, mats.shape[0] // group, body, 0)
+    out[...] = (acc[...] + dense[...]).astype(jnp.bfloat16)
 
 
 def place_tiles(source, dest, got, mats, acc):
     vmem = pl.BlockSpec(memory_space=pltpu.VMEM)
     smem = pl.BlockSpec(memory_space=pltpu.SMEM)
     return pl.pallas_call(
-        place_kernel,
+        functools.partial(place_kernel, lax.axis_size("row") // 2),
         out_shape=jax.ShapeDtypeStruct(acc.shape, jnp.bfloat16),
-        in_specs=[smem, smem, vmem, vmem, pl.BlockSpec(memory_space=pl.ANY)],
+        in_specs=[smem, smem, vmem, vmem, vmem],
         out_specs=vmem,
-        scratch_shapes=[pltpu.VMEM(acc.shape, jnp.float32), pltpu.SemaphoreType.DMA],
+        scratch_shapes=[pltpu.VMEM(acc.shape, jnp.float32)],
+        compiler_params=pltpu.CompilerParams(vmem_limit_bytes=20 * 2**20),
         name="place_tiles",
     )(source, dest, got, mats, acc)
 
@@ -388,7 +391,7 @@
             pltpu.SemaphoreType.DMA((30,)),
             pltpu.SemaphoreType.DMA((30,)),
         ],
-        compiler_params=pltpu.CompilerParams(collective_id=1, has_side_effects=True),
+        compiler_params=pltpu.CompilerParams(collective_id=1, has_side_effects=True, vmem_limit_bytes=10 * 2**20),
         name="scatter_and_project",
     )(part, weight, bias)
 
@@ -407,26 +410,17 @@
     out_bias,
 ):
     depth = lax.axis_size("row") // 2
-    block_rows = dense_blocks.shape[0]
-    me = lax.axis_index("row")
     got, acc, mats = gather_and_prepare(
         features,
-        dense_blocks.reshape(block_rows, 2 * FEAT),
+        dense_blocks,
         thick_neighbour_labels,
         entry_count[0],
         entry_rows[0, 0],
         entry_cols[0, 0],
-        edge_strength_list[0, 0].astype(jnp.float32),
+        edge_strength_list[0, 0],
     )
-    half = depth // 2
-    block = tile_source[0] // 2
-    offset = (block // 2 - me // 2 + half - 1 + depth) % depth - (half - 1)
-    near_place = offset + NEAR
-    far_place = 2 * NEAR + 1 + jnp.where(offset < 0, offset + half - 1, offset + half - 2 - 2 * NEAR)
-    place = jnp.where(jnp.abs(offset) <= NEAR, near_place, far_place)
-    source = (place * 2 + (block + me) % 2) * 2 + tile_source[0] % 2
     part = place_tiles(
-        source.astype(jnp.int32),
+        tile_source[0],
         tile_dest[0],
         got.reshape(4 * depth, TILE, FEAT),
         mats,

time: 104 us -> 89.8 us (0.86)
  Pallas kernels: 94.3 us -> 81.7 us
  other arithmetic: 2.78 us -> 0 us
  local copies, waits for them, and re-layouts: 6.46 us -> 7.75 us
    pallas_call x1, Pallas kernels: 16.4 us -> 5.32 us  [place_tiles(): pl.pallas_call(functools.partial(place_kernel, lax.axis_size('row') // 2)...]
    convert_element_type x1 -> x0, other arithmetic: 1.5 us -> none  [shards(): edge_strength_list[0, 0].astype(jnp.float32)]
    unnamed x2 -> x23, local copies, waits for them, and re-layouts: 6.46 us -> 7.75 us
    add x1 -> x0, other arithmetic: 1.28 us -> none  [shards(): source = (place * 2 + (block + me) % 2) * 2 + tile_source[0] % 2]
    pallas_call x1, Pallas kernels: 26.6 us -> 25.4 us  [scatter_and_project(): pl.pallas_call(scatter_kernel, out_shape=jax.ShapeDtypeStruct((2 * TILE,...]
where the time goes in v2:
time: 89.8 us; the launch traced here: 89.5 us
  Pallas kernels  81.7 us (91%)
  local copies, waits for them, and re-layouts  7.75 us (9%)
    pallas_call x1, Pallas kernels, gather_and_prepare(): pl.pallas_call(functools.partial(gather_kernel, depth), out_shape=(jax.Sh...  51 us
    pallas_call x1, Pallas kernels, scatter_and_project(): pl.pallas_call(scatter_kernel, out_shape=jax.ShapeDtypeStruct((2 * TILE,...  25.4 us
    unnamed x23, local copies, waits for them, and re-layouts  7.75 us
    pallas_call x1, Pallas kernels, place_tiles(): pl.pallas_call(functools.partial(place_kernel, lax.axis_size('row') // 2)...  5.32 us

profile of v2, /device:TPU:1, one launch (start us, length us, event | category | flops | bytes accessed | tf_op | source)
XLA Modules:
  0.0 89.5 jit_solution(4371778131187897675)
XLA Ops:
  0.0 0.0 copy-start.10
  0.0 0.0 copy-start.9
  0.0 0.0 copy-start
  0.0 2.2 %copy-done = bf16[4096,2,256]{2,1,0:T(2,128)(2,1)S(1)} copy-done((bf16[4096,2,256]{2,1,0:T(2,128)(2,1)S(1)}, bf16[4096,2,256]{2,1,0:T(2,128)(2,1)}, u32[]{:S(2)}) %copy-start) | copy-done | bytes 4194328
  2.2 0.0 copy-start.1
  2.2 0.9 %copy-done.1 = bf16[256,256]{1,0:T(8,128)(2,1)S(1)} copy-done((bf16[256,256]{1,0:T(8,128)(2,1)S(1)}, bf16[256,256]{1,0:T(8,128)(2,1)}, u32[]{:S(2)}) %copy-start.1) | copy-done | bytes 131096
  3.1 0.0 copy-start.2
  3.1 0.9 %copy-done.2 = s32[1,1,64,512]{3,2,1,0:T(8,128)S(1)} copy-done((s32[1,1,64,512]{3,2,1,0:T(8,128)S(1)}, s32[1,1,64,512]{3,2,1,0:T(8,128)}, u32[]{:S(2)}) %copy-start.2) | copy-done | bytes 131096
  4.0 0.0 copy-start.3
  4.0 0.9 %copy-done.3 = s32[1,1,64,512]{3,2,1,0:T(8,128)S(1)} copy-done((s32[1,1,64,512]{3,2,1,0:T(8,128)S(1)}, s32[1,1,64,512]{3,2,1,0:T(8,128)}, u32[]{:S(2)}) %copy-start.3) | copy-done | bytes 131096
  4.9 0.0 copy-start.5
  4.9 0.8 copy-done.5
  5.8 0.0 copy-start.7
  5.8 0.7 copy-done.7
  6.4 0.0 copy-start.8
  6.4 0.7 copy-done.8
  7.1 51.0 %gather_and_prepare.1 = (bf16[32,256,256]{2,1,0:T(8,128)(2,1)S(1)}, f32[4096,256]{1,0:T(8,128)S(1)}, bf16[64,128,128]{2,1,0:T(8,128)(2,1)S(1)}) custom-call(s32[1,2]{1,0:T(1,128)S(1)} %copy-done.7, s32[1,64]{1,0:T(1,128)S(1)} %bitcast.13, bf16[256,256]{1,0:T(8,128)(2,1)S(1)} %copy-done.1, s32[64,512]{1,0:T(8,128)S(1)} %bitcast.9, s32[64,512]{1,0:T(8,128)S(1)} %bitcast.10, ...), custom_call_target="tpu_custom_call" | custom-call | tf_op jit(solution)/shard_map/gather_and_prepare/pallas_call | solution.py:196
  58.0 0.0 copy-done.10
  58.1 0.0 copy-done.9
  58.1 0.0 copy-start.4
  58.1 0.0 copy-start.6
  58.1 5.3 %place_tiles.1.part = bf16[4096,256]{1,0:T(8,128)(2,1)S(1)} custom-call(s32[1,64]{1,0:T(1,128)S(1)} %bitcast.14, s32[1,64]{1,0:T(1,128)S(1)} %bitcast.15, bf16[64,128,256]{2,1,0:T(8,128)(2,1)S(1)} %bitcast.8, bf16[64,128,128]{2,1,0:T(8,128)(2,1)S(1)} %get-tuple-element.9.mats, f32[4096,256]{1,0:T(8,128)S(1)} %get-tuple-element.10.dense), custom_call_target="tpu_custom_call" | custom-call | tf_op jit(solution)/shard_map/place_tiles/pallas_call | solution.py:248
  63.4 0.0 copy-done.4
  63.4 0.0 copy-done.6
  63.4 25.4 %scatter_and_project.1 = bf16[256,256]{1,0:T(8,128)(2,1)S(1)} custom-call(bf16[4096,256]{1,0:T(8,128)(2,1)S(1)} %place_tiles.1.part, bf16[256,256]{1,0:T(8,128)(2,1)S(1)} %copy-done.4, f32[1,256]{1,0:T(1,128)S(1)} %bitcast.12), custom_call_target="tpu_custom_call" | custom-call | tf_op jit(solution)/shard_map/scatter_and_project/pallas_call | solution.py:378
  88.8 0.7 copy.13
Async XLA Ops:
  0.0 58.1 %copy-start.10 = (s32[1,1,64]{2,1,0:T(1,128)S(1)}, s32[1,1,64]{2,1,0:T(1,128)}, u32[]{:S(2)}) copy-start(s32[1,1,64]{2,1,0:T(1,128)} %param.15) | copy-start | bytes 772
  0.0 58.1 %copy-start.9 = (s32[1,1,64]{2,1,0:T(1,128)S(1)}, s32[1,1,64]{2,1,0:T(1,128)}, u32[]{:S(2)}) copy-start(s32[1,1,64]{2,1,0:T(1,128)} %param.14) | copy-start | bytes 772
  0.0 2.2 %copy-start = (bf16[4096,2,256]{2,1,0:T(2,128)(2,1)S(1)}, bf16[4096,2,256]{2,1,0:T(2,128)(2,1)}, u32[]{:S(2)}) copy-start(bf16[4096,2,256]{2,1,0:T(2,128)(2,1)} %dense_v.1) | copy-start | bytes 12582916
  2.2 0.9 %copy-start.1 = (bf16[256,256]{1,0:T(8,128)(2,1)S(1)}, bf16[256,256]{1,0:T(8,128)(2,1)}, u32[]{:S(2)}) copy-start(bf16[256,256]{1,0:T(8,128)(2,1)} %feat.1) | copy-start | bytes 393220
  3.1 0.9 %copy-start.2 = (s32[1,1,64,512]{3,2,1,0:T(8,128)S(1)}, s32[1,1,64,512]{3,2,1,0:T(8,128)}, u32[]{:S(2)}) copy-start(s32[1,1,64,512]{3,2,1,0:T(8,128)} %param.16) | copy-start | bytes 393220
  4.0 0.9 %copy-start.3 = (s32[1,1,64,512]{3,2,1,0:T(8,128)S(1)}, s32[1,1,64,512]{3,2,1,0:T(8,128)}, u32[]{:S(2)}) copy-start(s32[1,1,64,512]{3,2,1,0:T(8,128)} %param.17) | copy-start | bytes 393220
  4.9 0.8 copy-start.5
  5.8 0.7 copy-start.7
  6.4 0.7 copy-start.8
  58.1 5.3 %copy-start.4 = (bf16[256,256]{1,0:T(8,128)(2,1)S(1)}, bf16[256,256]{1,0:T(8,128)(2,1)}, u32[]{:S(2)}) copy-start(bf16[256,256]{1,0:T(8,128)(2,1)} %weight.1) | copy-start | bytes 393220
  58.1 5.3 %copy-start.6 = (f32[256]{0:T(256)S(1)}, f32[256]{0:T(256)}, u32[]{:S(2)}) copy-start(f32[256]{0:T(256)} %param.21) | copy-start | bytes 3076

commit v3 on v2

--- a/solution.py
+++ b/solution.py
@@ -23,15 +23,17 @@
     rows_ref,
     cols_ref,
     strength_in,
-    dense_v,
+    dense_hbm,
     got,
     acc_v,
     mats_v,
     panels,
     mixed,
     strength,
+    dense_v,
     send_sem,
     recv_sem,
+    local_sem,
 ):
     me = lax.axis_index("row")
     z = me // 2
@@ -48,6 +50,8 @@
     for peer in (mate,) + ring:
         pl.semaphore_signal(barrier, inc=1, device_id=peer, device_id_type=MESH)
 
+    dense_in = pltpu.make_async_copy(dense_hbm, dense_v, local_sem)
+    dense_in.start()
     got[2 * (half - 1)] = feat[...]
     strength[...] = strength_in[...].astype(jnp.float32)
     pl.semaphore_wait(barrier, 3)
@@ -151,8 +155,8 @@
         begin(ring_copy(2, way, 1))
 
     tiles = mats_v.shape[0]
-    early = 3 * (NEAR + 1)
-    late = 3 * (half - NEAR - 1)
+    early = 2 * half
+    late = half
     slot = 0
     for step in range(1, half + 1):
         for piece in range(3):
@@ -165,6 +169,7 @@
                         for sign in step_sign:
                             mate_copy(-sign * near_step, 0).wait_recv()
                     fetch_panels()
+                    dense_in.wait()
                 dense_part((slot - early) * chunks // late, (slot - early + 1) * chunks // late)
             for way in (0, 1):
                 if step <= last[piece][way]:
@@ -196,20 +201,22 @@
     return pl.pallas_call(
         functools.partial(gather_kernel, depth),
         out_shape=(
-            jax.ShapeDtypeStruct((2 * depth, FEAT, FEAT), jnp.bfloat16),
-            jax.ShapeDtypeStruct((block_rows, FEAT), jnp.float32),
-            jax.ShapeDtypeStruct((tiles, TILE, TILE), jnp.bfloat16),
+            pltpu.VMEM((2 * depth, FEAT, FEAT), jnp.bfloat16),
+            pltpu.VMEM((block_rows, FEAT), jnp.float32),
+            pltpu.VMEM((tiles, TILE, TILE), jnp.bfloat16),
         ),
-        in_specs=[smem, smem, vmem, vmem, vmem, vmem, vmem],
+        in_specs=[smem, smem, vmem, vmem, vmem, vmem, pl.BlockSpec(memory_space=pl.ANY)],
         out_specs=(vmem, vmem, vmem),
         scratch_shapes=[
             pltpu.VMEM((FEAT, 2 * FEAT), jnp.bfloat16),
             pltpu.VMEM((4, 2 * FEAT, TILE), jnp.float32),
             pltpu.VMEM(rows.shape, jnp.float32),
+            pltpu.VMEM(dense_blocks.shape, jnp.bfloat16),
             pltpu.SemaphoreType.DMA((sems,)),
             pltpu.SemaphoreType.DMA((sems,)),
+            pltpu.SemaphoreType.DMA,
         ],
-        compiler_params=pltpu.CompilerParams(collective_id=0, has_side_effects=True, vmem_limit_bytes=20 * 2**20),
+        compiler_params=pltpu.CompilerParams(collective_id=0, has_side_effects=True, vmem_limit_bytes=67043328 - 10 * 2**20 - 65536),
         name="gather_and_prepare",
     )(labels, counts, features, rows, cols, strength, dense_blocks)
 

time: 89.8 us -> 82.9 us (0.923)
  local copies, waits for them, and re-layouts: 7.75 us -> 0.68 us
    unnamed x23 -> x9, local copies, waits for them, and re-layouts: 7.75 us -> 0.68 us
where the time goes in v3:
time: 82.9 us; the launch traced here: 82.8 us
  Pallas kernels  82 us (99%)
    pallas_call x1, Pallas kernels, gather_and_prepare(): pl.pallas_call(functools.partial(gather_kernel, depth), out_shape=(pltpu....  50.9 us
    pallas_call x1, Pallas kernels, scatter_and_project(): pl.pallas_call(scatter_kernel, out_shape=jax.ShapeDtypeStruct((2 * TILE,...  26.1 us
    pallas_call x1, Pallas kernels, place_tiles(): pl.pallas_call(functools.partial(place_kernel, lax.axis_size('row') // 2)...  4.97 us

profile of v3, /device:TPU:1, one launch (start us, length us, event | category | flops | bytes accessed | tf_op | source)
XLA Modules:
  0.0 82.8 jit_solution(4043310816541700482)
XLA Ops:
  0.0 0.0 copy-start.3
  0.0 0.0 copy-start.2
  0.0 50.9 %gather_and_prepare.1 = (bf16[32,256,256]{2,1,0:T(8,128)(2,1)S(1)}, f32[4096,256]{1,0:T(8,128)S(1)}, bf16[64,128,128]{2,1,0:T(8,128)(2,1)S(1)}) custom-call(s32[1,2]{1,0:T(1,128)} %labels.1, s32[1,64]{1,0:T(1,128)} %bitcast.15, bf16[256,256]{1,0:T(8,128)(2,1)} %feat.1, s32[64,512]{1,0:T(8,128)} %bitcast.12, s32[64,512]{1,0:T(8,128)} %bitcast.13, ...), custom_call_target="tpu_custom_call" | custom-call | tf_op jit(solution)/shard_map/gather_and_prepare/pallas_call | solution.py:201
  50.9 0.0 copy-done.3
  51.0 0.0 copy-done.2
  51.0 0.0 copy-start
  51.0 0.0 copy-start.1
  51.0 5.0 %place_tiles.1.part = bf16[4096,256]{1,0:T(8,128)(2,1)S(1)} custom-call(s32[1,64]{1,0:T(1,128)S(1)} %bitcast.10, s32[1,64]{1,0:T(1,128)S(1)} %bitcast.11, bf16[64,128,256]{2,1,0:T(8,128)(2,1)S(1)} %bitcast.8, bf16[64,128,128]{2,1,0:T(8,128)(2,1)S(1)} %get-tuple-element.9.mats, f32[4096,256]{1,0:T(8,128)S(1)} %get-tuple-element.10.dense), custom_call_target="tpu_custom_call" | custom-call | tf_op jit(solution)/shard_map/place_tiles/pallas_call | solution.py:255
  56.0 0.0 copy-done
  56.0 0.0 copy-done.1
  56.0 26.1 %scatter_and_project.1 = bf16[256,256]{1,0:T(8,128)(2,1)S(1)} custom-call(bf16[4096,256]{1,0:T(8,128)(2,1)S(1)} %place_tiles.1.part, bf16[256,256]{1,0:T(8,128)(2,1)S(1)} %copy-done, f32[1,256]{1,0:T(1,128)S(1)} %bitcast.9), custom_call_target="tpu_custom_call" | custom-call | tf_op jit(solution)/shard_map/scatter_and_project/pallas_call | solution.py:385
  82.1 0.7 copy.13
Async XLA Ops:
  0.0 50.9 %copy-start.3 = (s32[1,1,64]{2,1,0:T(1,128)S(1)}, s32[1,1,64]{2,1,0:T(1,128)}, u32[]{:S(2)}) copy-start(s32[1,1,64]{2,1,0:T(1,128)} %param.15) | copy-start | bytes 772
  0.0 50.9 %copy-start.2 = (s32[1,1,64]{2,1,0:T(1,128)S(1)}, s32[1,1,64]{2,1,0:T(1,128)}, u32[]{:S(2)}) copy-start(s32[1,1,64]{2,1,0:T(1,128)} %param.14) | copy-start | bytes 772
  51.0 5.0 %copy-start = (bf16[256,256]{1,0:T(8,128)(2,1)S(1)}, bf16[256,256]{1,0:T(8,128)(2,1)}, u32[]{:S(2)}) copy-start(bf16[256,256]{1,0:T(8,128)(2,1)} %weight.1) | copy-start | bytes 393220
  51.0 5.0 %copy-start.1 = (f32[256]{0:T(256)S(1)}, f32[256]{0:T(256)}, u32[]{:S(2)}) copy-start(f32[256]{0:T(256)} %param.21) | copy-start | bytes 3076

commit v4 on v3

--- a/solution.py
+++ b/solution.py
@@ -173,15 +173,18 @@
                 dense_part((slot - early) * chunks // late, (slot - early + 1) * chunks // late)
             for way in (0, 1):
                 if step <= last[piece][way]:
+                    if piece == 2 and step in BY_MATE:
+                        continue
                     away = -step_sign[way] * step
-                    if piece == 2 and step in BY_MATE:
-                        mate_copy(away, 1).wait_recv()
-                    else:
-                        ring_copy(piece, way, step).wait_recv()
+                    ring_copy(piece, way, step).wait_recv()
                     if step < last[piece][way] and not (piece == 2 and step + 1 in BY_MATE):
                         begin(ring_copy(piece, way, step + 1))
                     if piece == 0 or piece == 1 and step in BY_MATE:
                         begin(mate_copy(away, piece))
+            if piece == 0 and step - 1 in BY_MATE:
+                for way in (0, 1):
+                    mate_copy(-step_sign[way] * (step - 1), 1).wait_recv()
+                    begin(ring_copy(2, way, step))
             slot += 1
     for offset in range(NEAR + 1, half + 1):
         mate_copy(offset, 0).wait_recv()
@@ -327,22 +330,16 @@
         copy.start()
         started.append(copy)
 
-    first_order = [(h, q, t) for t in (0, 1) for q in (1, 0) for h in (0, 1)]
-    sends_one = [(h, q, 2 if k == 0 else HALVES[h][0]) for (h, q, k) in first_order]
-    stays = [(h, q, HALVES[h][1]) for q in (1, 0) for h in (0, 1)]
-    ends = [(h, q, 0) for q in (1, 0) for h in (0, 1)]
-    for key in sends_one + stays + ends:
-        begin(core_copy(*key))
-    for h, q, t in sends_one:
+    def send_one(h, q, t):
         copy = one_copy(h, q, t)
         core_copy(h, q, t).wait_recv()
-        way = HALVES[h][0]
-        slot = (h * 2 + q) * 2 + (0 if t == way else 1)
+        slot = (h * 2 + q) * 2 + (0 if t == HALVES[h][0] else 1)
         sum_core[slot] = (
             wide(piece(h, q, t, core)) + wide(from_core.at[number(h, q, t)])
         ).astype(jnp.bfloat16)
         begin(copy)
-    for h, q, t in stays:
+
+    def send_two(h, q, t):
         core_copy(h, q, t).wait_recv()
         one_copy(h, q, 2).wait_recv()
         sum_two[h * 2 + q] = (
@@ -351,6 +348,25 @@
             + wide(from_one.at[(h * 2 + q) * 2 + 1])
         ).astype(jnp.bfloat16)
         begin(two_copy(h, q))
+
+    plan = []
+    for send, q, place in (
+        (send_one, 1, None),
+        (send_one, 1, 0),
+        (send_one, 0, None),
+        (send_two, 1, 1),
+        (send_one, 0, 0),
+        (send_two, 0, 1),
+    ):
+        for h in (0, 1):
+            plan.append((send, (h, q, 2 if place is None else HALVES[h][place])))
+    for send, key in plan:
+        begin(core_copy(*key))
+    for q in (1, 0):
+        for h in (0, 1):
+            begin(core_copy(h, q, 0))
+    for send, key in plan:
+        send(*key)
 
     def total(h, q):
         core_copy(h, q, 0).wait_recv()

time: 82.9 us -> 81.3 us (0.981)
  Pallas kernels: 82 us -> 80.4 us
    pallas_call x1, Pallas kernels: 50.9 us -> 48.8 us  [gather_and_prepare(): pl.pallas_call(functools.partial(gather_kernel, depth), out_shape=(pltpu....]
where the time goes in v4:
time: 81.3 us; the launch traced here: 81.1 us
  Pallas kernels  80.4 us (99%)
    pallas_call x1, Pallas kernels, gather_and_prepare(): pl.pallas_call(functools.partial(gather_kernel, depth), out_shape=(pltpu....  48.8 us
    pallas_call x1, Pallas kernels, scatter_and_project(): pl.pallas_call(scatter_kernel, out_shape=jax.ShapeDtypeStruct((2 * TILE,...  26.7 us
    pallas_call x1, Pallas kernels, place_tiles(): pl.pallas_call(functools.partial(place_kernel, lax.axis_size('row') // 2)...  4.97 us

profile of v4, /device:TPU:1, one launch (start us, length us, event | category | flops | bytes accessed | tf_op | source)
XLA Modules:
  0.0 81.1 jit_solution(1646953192998042255)
XLA Ops:
  0.0 0.0 copy-start.3
  0.0 0.0 copy-start.2
  0.0 48.8 %gather_and_prepare.1 = (bf16[32,256,256]{2,1,0:T(8,128)(2,1)S(1)}, f32[4096,256]{1,0:T(8,128)S(1)}, bf16[64,128,128]{2,1,0:T(8,128)(2,1)S(1)}) custom-call(s32[1,2]{1,0:T(1,128)} %labels.1, s32[1,64]{1,0:T(1,128)} %bitcast.15, bf16[256,256]{1,0:T(8,128)(2,1)} %feat.1, s32[64,512]{1,0:T(8,128)} %bitcast.12, s32[64,512]{1,0:T(8,128)} %bitcast.13, ...), custom_call_target="tpu_custom_call" | custom-call | tf_op jit(solution)/shard_map/gather_and_prepare/pallas_call | solution.py:204
  48.8 0.0 copy-done.3
  48.8 0.0 copy-done.2
  48.8 0.0 copy-start
  48.8 0.0 copy-start.1
  48.8 5.0 %place_tiles.1.part = bf16[4096,256]{1,0:T(8,128)(2,1)S(1)} custom-call(s32[1,64]{1,0:T(1,128)S(1)} %bitcast.10, s32[1,64]{1,0:T(1,128)S(1)} %bitcast.11, bf16[64,128,256]{2,1,0:T(8,128)(2,1)S(1)} %bitcast.8, bf16[64,128,128]{2,1,0:T(8,128)(2,1)S(1)} %get-tuple-element.9.mats, f32[4096,256]{1,0:T(8,128)S(1)} %get-tuple-element.10.dense), custom_call_target="tpu_custom_call" | custom-call | tf_op jit(solution)/shard_map/place_tiles/pallas_call | solution.py:258
  53.8 0.0 copy-done
  53.8 0.0 copy-done.1
  53.8 26.7 %scatter_and_project.1 = bf16[256,256]{1,0:T(8,128)(2,1)S(1)} custom-call(bf16[4096,256]{1,0:T(8,128)(2,1)S(1)} %place_tiles.1.part, bf16[256,256]{1,0:T(8,128)(2,1)S(1)} %copy-done, f32[1,256]{1,0:T(1,128)S(1)} %bitcast.9), custom_call_target="tpu_custom_call" | custom-call | tf_op jit(solution)/shard_map/scatter_and_project/pallas_call | solution.py:401
  80.5 0.7 copy.13
Async XLA Ops:
  0.0 48.8 %copy-start.3 = (s32[1,1,64]{2,1,0:T(1,128)S(1)}, s32[1,1,64]{2,1,0:T(1,128)}, u32[]{:S(2)}) copy-start(s32[1,1,64]{2,1,0:T(1,128)} %param.15) | copy-start | bytes 772
  0.0 48.8 %copy-start.2 = (s32[1,1,64]{2,1,0:T(1,128)S(1)}, s32[1,1,64]{2,1,0:T(1,128)}, u32[]{:S(2)}) copy-start(s32[1,1,64]{2,1,0:T(1,128)} %param.14) | copy-start | bytes 772
  48.8 5.0 %copy-start = (bf16[256,256]{1,0:T(8,128)(2,1)S(1)}, bf16[256,256]{1,0:T(8,128)(2,1)}, u32[]{:S(2)}) copy-start(bf16[256,256]{1,0:T(8,128)(2,1)} %weight.1) | copy-start | bytes 393220
  48.8 5.0 %copy-start.1 = (f32[256]{0:T(256)S(1)}, f32[256]{0:T(256)}, u32[]{:S(2)}) copy-start(f32[256]{0:T(256)} %param.21) | copy-start | bytes 3076

commit v5 on v4

--- a/solution.py
+++ b/solution.py
@@ -10,7 +10,7 @@
 FEAT = 256
 TILE = 128
 NEAR = 2
-BY_MATE = (4, 6)
+BY_MATE = (5,)
 MESH = pl.DeviceIdType.MESH
 HALVES = ((1, 3), (3, 1))
 
@@ -228,7 +228,7 @@
     acc[...] = jnp.zeros_like(acc)
     me = lax.axis_index("row")
     half = depth // 2
-    group = 4
+    group = 8
 
     def spot(i):
         listed = source[0, i]

time: 81.3 us -> 78.4 us (0.964)
  Pallas kernels: 80.4 us -> 77.5 us
    pallas_call x1, Pallas kernels: 4.97 us -> 3.65 us  [place_tiles(): pl.pallas_call(functools.partial(place_kernel, lax.axis_size('row') // 2)...]
    pallas_call x1, Pallas kernels: 26.7 us -> 25.5 us  [scatter_and_project(): pl.pallas_call(scatter_kernel, out_shape=jax.ShapeDtypeStruct((2 * TILE,...]
where the time goes in v5:
time: 78.4 us; the launch traced here: 78.3 us
  Pallas kernels  77.5 us (99%)
    pallas_call x1, Pallas kernels, gather_and_prepare(): pl.pallas_call(functools.partial(gather_kernel, depth), out_shape=(pltpu....  48.4 us
    pallas_call x1, Pallas kernels, scatter_and_project(): pl.pallas_call(scatter_kernel, out_shape=jax.ShapeDtypeStruct((2 * TILE,...  25.5 us
    pallas_call x1, Pallas kernels, place_tiles(): pl.pallas_call(functools.partial(place_kernel, lax.axis_size('row') // 2)...  3.65 us

profile of v5, /device:TPU:1, one launch (start us, length us, event | category | flops | bytes accessed | tf_op | source)
XLA Modules:
  0.0 78.3 jit_solution(14981813015347443152)
XLA Ops:
  0.0 0.0 copy-start.3
  0.0 0.0 copy-start.2
  0.0 48.4 %gather_and_prepare.1 = (bf16[32,256,256]{2,1,0:T(8,128)(2,1)S(1)}, f32[4096,256]{1,0:T(8,128)S(1)}, bf16[64,128,128]{2,1,0:T(8,128)(2,1)S(1)}) custom-call(s32[1,2]{1,0:T(1,128)} %labels.1, s32[1,64]{1,0:T(1,128)} %bitcast.15, bf16[256,256]{1,0:T(8,128)(2,1)} %feat.1, s32[64,512]{1,0:T(8,128)} %bitcast.12, s32[64,512]{1,0:T(8,128)} %bitcast.13, ...), custom_call_target="tpu_custom_call" | custom-call | tf_op jit(solution)/shard_map/gather_and_prepare/pallas_call | solution.py:204
  48.4 0.0 copy-done.3
  48.4 0.0 copy-done.2
  48.4 0.0 copy-start
  48.4 0.0 copy-start.1
  48.4 3.6 %place_tiles.1.part = bf16[4096,256]{1,0:T(8,128)(2,1)S(1)} custom-call(s32[1,64]{1,0:T(1,128)S(1)} %bitcast.10, s32[1,64]{1,0:T(1,128)S(1)} %bitcast.11, bf16[64,128,256]{2,1,0:T(8,128)(2,1)S(1)} %bitcast.8, bf16[64,128,128]{2,1,0:T(8,128)(2,1)S(1)} %get-tuple-element.9.mats, f32[4096,256]{1,0:T(8,128)S(1)} %get-tuple-element.10.dense), custom_call_target="tpu_custom_call" | custom-call | tf_op jit(solution)/shard_map/place_tiles/pallas_call | solution.py:258
  52.1 0.0 copy-done
  52.1 0.0 copy-done.1
  52.1 25.5 %scatter_and_project.1 = bf16[256,256]{1,0:T(8,128)(2,1)S(1)} custom-call(bf16[4096,256]{1,0:T(8,128)(2,1)S(1)} %place_tiles.1.part, bf16[256,256]{1,0:T(8,128)(2,1)S(1)} %copy-done, f32[1,256]{1,0:T(1,128)S(1)} %bitcast.9), custom_call_target="tpu_custom_call" | custom-call | tf_op jit(solution)/shard_map/scatter_and_project/pallas_call | solution.py:401
  77.6 0.7 copy.13
Async XLA Ops:
  0.0 48.4 %copy-start.3 = (s32[1,1,64]{2,1,0:T(1,128)S(1)}, s32[1,1,64]{2,1,0:T(1,128)}, u32[]{:S(2)}) copy-start(s32[1,1,64]{2,1,0:T(1,128)} %param.15) | copy-start | bytes 772
  0.0 48.4 %copy-start.2 = (s32[1,1,64]{2,1,0:T(1,128)S(1)}, s32[1,1,64]{2,1,0:T(1,128)}, u32[]{:S(2)}) copy-start(s32[1,1,64]{2,1,0:T(1,128)} %param.14) | copy-start | bytes 772
  48.4 3.7 %copy-start = (bf16[256,256]{1,0:T(8,128)(2,1)S(1)}, bf16[256,256]{1,0:T(8,128)(2,1)}, u32[]{:S(2)}) copy-start(bf16[256,256]{1,0:T(8,128)(2,1)} %weight.1) | copy-start | bytes 393220
  48.4 3.7 %copy-start.1 = (f32[256]{0:T(256)S(1)}, f32[256]{0:T(256)}, u32[]{:S(2)}) copy-start(f32[256]{0:T(256)} %param.21) | copy-start | bytes 3076
